TPU v7x, 32 devices: a whole 2x2x4 slice. The times are simulated.
32 devices in a mesh: seq: 16 (over z, y, x), head: 2 (over core).
Axes of the slice: x: 2, y: 2, z: 4, core: 2. Of those that a mesh axis runs over, the one named last changes fastest.
Arguments:
- raw_keys: bfloat16 [2, 16384, 8, 128], P(None, 'seq', 'head'), may hold values from -6 to 6
- raw_values: bfloat16 [2, 16384, 8, 128], P(None, 'seq', 'head'), may hold values from -6 to 6
- phase: int32 [2], replicated, may hold values from 0 to 255, as said below
- ratio: int32 [2, 16], replicated, may hold values from 8 to 32, as said below
- resident_len: int32 [2, 16], replicated, may hold values from 1 to 256, as said below
- beacon_queries: bfloat16 [2, 2048, 8, 8, 128], P(None, 'seq', 'head'), may hold values from -150 to 150
- beacon_wk: bfloat16 [8192, 1024], P('seq', 'head'), may hold values from -0.125 to 0.125
- beacon_wv: bfloat16 [8192, 1024], P('seq', 'head'), may hold values from -0.125 to 0.125
- resident_keys: bfloat16 [2, 4096, 8, 128], P(None, 'seq', 'head'), may hold values from -6 to 6
- resident_values: bfloat16 [2, 4096, 8, 128], P(None, 'seq', 'head'), may hold values from -6 to 6
- decode_queries: bfloat16 [4, 2, 8, 8, 128], P(None, None, 'head'), may hold values from -150 to 150
- out_weight: bfloat16 [8192, 8192], P('head', 'seq'), may hold values from -0.0625 to 0.0625
Outputs:
- beacon_keys: bfloat16 [2, 2048, 8, 128], P(None, 'seq', 'head')
- beacon_values: bfloat16 [2, 2048, 8, 128], P(None, 'seq', 'head')
- projected: bfloat16 [4, 2, 8192], P(None, None, 'seq')
Inputs may be any that keep to these rules, and one draw needn't show every extreme that they name: `phase`: some request has 255. `ratio`: each value is 1024 // 128 times 1, 2 or 4; both ends occur. `resident_len`: some pair has 256.
All inputs are finite; a program needn't handle non-finite values.
Results may differ from a plain program's by a relative error of at most 0.025.
Values may be sent and summed in bfloat16 or wider, within the bound.
A program may use at most 64 MiB of HBM per device.

v0:
```python
import math
import jax
import jax.numpy as jnp
from jax import lax
from jax.sharding import PartitionSpec as P

G = 8
INTERVAL = 1024
NB = 128
OFF = 256
STEPS = 4
masked_score = -1e30


def shifted(value, axis, steps):
    count = lax.axis_size(axis)
    first, last = (max(0, -steps), min(count, count - steps))
    return lax.ppermute(value, axis, [(source, source + steps) for source in range(first, last)])


def joined(shard, axis, combine):
    everything = jax.tree.map(lambda part: lax.all_gather(part, axis), shard)
    first = jax.tree.map(lambda part: part[0], everything)

    def hop(k, so_far):
        return combine(so_far, jax.tree.map(lambda part: part[k], everything))

    return lax.fori_loop(1, lax.axis_size(axis), hop, first)


def blend(former, latter):
    row_peak = jnp.maximum(former[0], latter[0])
    former_scale = jnp.exp(former[0] - row_peak)
    latter_scale = jnp.exp(latter[0] - row_peak)
    weight_sum = former[1] * former_scale + latter[1] * latter_scale
    weighted = former[2] * former_scale[..., None] + latter[2] * latter_scale[..., None]
    return (row_peak, weight_sum, weighted)


def pool_part(queries, key_rows, value_rows, positions, present, reaches):
    inv_root = 1.0 / math.sqrt(queries.shape[-1])

    def per_request(members):
        query_block, key_block, value_block, position_row, present_row, reach_row = members
        scores = (
            jnp.einsum("jkgd,ikd->jkgi", query_block, key_block, preferred_element_type=jnp.float32)
            * inv_root
        )
        allowed = (
            present_row[None, :]
            & (position_row[None, :] >= 0)
            & (position_row[None, :] < INTERVAL)
            & (position_row[None, :] < reach_row[:, None])
        )
        cache_mask = allowed[:, None, None, :]
        row_peak = jnp.max(jnp.where(cache_mask, scores, masked_score), axis=-1)
        weights = jnp.where(cache_mask, jnp.exp(scores - row_peak[..., None]), 0.0)
        weight_sum = jnp.sum(weights, axis=-1)
        weighted = jnp.einsum(
            "jkgi,ikd->jkgd",
            weights.astype(jnp.bfloat16),
            value_block,
            preferred_element_type=jnp.float32,
        )
        return (row_peak, weight_sum, weighted)

    return lax.map(per_request, (queries, key_rows, value_rows, positions, present, reaches))


def body(
    raw_keys,
    raw_values,
    phase,
    ratio,
    resident_len,
    beacon_queries,
    beacon_wk,
    beacon_wv,
    resident_keys,
    resident_values,
    decode_queries,
    out_weight,
):
    requests = raw_keys.shape[0]
    kv_local = raw_keys.shape[2]
    head_dim = raw_keys.shape[3]
    shard_index = lax.axis_index("seq")
    shard_count = lax.axis_size("seq")
    is_first = shard_index == 0
    is_last = shard_index == shard_count - 1
    own_ratio = lax.dynamic_index_in_dim(ratio, shard_index, 1, keepdims=False)
    slot_ids = jnp.arange(NB, dtype=jnp.int32)
    lead_in = jnp.where(is_first, phase, 0)
    reaches = (slot_ids[None, :] + 1) * own_ratio[:, None] + lead_in[:, None]
    tail_keys = raw_keys[:, INTERVAL - OFF :]
    tail_values = raw_values[:, INTERVAL - OFF :]
    own_positions = jnp.arange(INTERVAL, dtype=jnp.int32)[None, :] + phase[:, None]
    rim_ids = jnp.arange(OFF, dtype=jnp.int32)
    rim_positions = rim_ids[None, :] - OFF + phase[:, None]
    near_keys, near_values = shifted((tail_keys, tail_values), "seq", 1)
    key_rows = jnp.concatenate([near_keys, raw_keys], axis=1)
    value_rows = jnp.concatenate([near_values, raw_values], axis=1)
    positions = jnp.concatenate([rim_positions, own_positions], axis=1)
    present = jnp.logical_not(is_first) | (positions >= phase[:, None])
    pooled_parts = pool_part(beacon_queries, key_rows, value_rows, positions, present, reaches)
    pooled = (pooled_parts[2] / pooled_parts[1][..., None]).astype(jnp.bfloat16)
    pooled_flat = pooled.reshape(requests * NB, kv_local * G * head_dim)
    pooled_whole = lax.all_gather(pooled_flat, "head", axis=1, tiled=True)
    key_sum = jnp.dot(
        pooled_whole,
        lax.all_gather(beacon_wk, "seq", axis=0, tiled=True),
        preferred_element_type=jnp.float32,
    )
    value_sum = jnp.dot(
        pooled_whole,
        lax.all_gather(beacon_wv, "seq", axis=0, tiled=True),
        preferred_element_type=jnp.float32,
    )
    made_keys = key_sum
    made_values = value_sum
    made_keys = made_keys.reshape(requests, NB, kv_local, head_dim)
    made_values = made_values.reshape(requests, NB, kv_local, head_dim)
    slot_live = slot_ids[None, :] < (INTERVAL // own_ratio)[:, None]
    beacon_keys = jnp.where(slot_live[:, :, None, None], made_keys, 0.0).astype(jnp.bfloat16)
    beacon_values = jnp.where(slot_live[:, :, None, None], made_values, 0.0).astype(jnp.bfloat16)
    cache_keys = jnp.concatenate([resident_keys, beacon_keys, tail_keys], axis=1)
    cache_values = jnp.concatenate([resident_values, beacon_values, tail_values], axis=1)
    own_len = lax.dynamic_index_in_dim(resident_len, shard_index, 1, keepdims=False)
    resident_ok = jnp.arange(resident_keys.shape[1], dtype=jnp.int32)[None, :] < own_len[:, None]
    leftover_ok = (rim_ids[None, :] >= OFF - phase[:, None]) & is_last
    usable = jnp.concatenate([resident_ok, slot_live, leftover_ok], axis=1)
    inv_root = 1.0 / math.sqrt(head_dim)
    scores = (
        jnp.einsum(
            "srkgd,rikd->rksgi", decode_queries, cache_keys, preferred_element_type=jnp.float32
        )
        * inv_root
    )
    cache_mask = usable[:, None, None, None, :]
    row_peak = jnp.max(jnp.where(cache_mask, scores, masked_score), axis=-1)
    weights = jnp.where(cache_mask, jnp.exp(scores - row_peak[..., None]), 0.0)
    weight_sum = jnp.sum(weights, axis=-1)
    weighted = jnp.einsum(
        "rksgi,rikd->rksgd",
        weights.astype(jnp.bfloat16),
        cache_values,
        preferred_element_type=jnp.float32,
    )
    merged = joined((row_peak, weight_sum, weighted), "seq", blend)
    total_sum = merged[1]
    total_weighted = merged[2]
    attended = (total_weighted / total_sum[..., None]).astype(jnp.bfloat16)
    attended = jnp.transpose(attended, (2, 0, 1, 3, 4)).reshape(
        STEPS * requests, kv_local * G * head_dim
    )
    partial_value = jnp.dot(attended, out_weight, preferred_element_type=jnp.float32)
    summed = lax.psum(partial_value, "head")
    projected = summed.astype(jnp.bfloat16).reshape(STEPS, requests, out_weight.shape[1])
    return (beacon_keys, beacon_values, projected)


def solution(mesh):
    return jax.shard_map(
        body,
        mesh=mesh,
        in_specs=(
            P(None, "seq", "head", None),
            P(None, "seq", "head", None),
            P(),
            P(),
            P(),
            P(None, "seq", "head", None, None),
            P("seq", "head"),
            P("seq", "head"),
            P(None, "seq", "head", None),
            P(None, "seq", "head", None),
            P(None, None, "head", None, None),
            P("head", "seq"),
        ),
        out_specs=(
            P(None, "seq", "head", None),
            P(None, "seq", "head", None),
            P(None, None, "seq"),
        ),
        check_vma=False,
    )
```

profile of v0, /device:TPU:0, one launch (start us, length us, event | category | flops | bytes accessed | tf_op | source)
XLA Modules:
  0.0 473.2 jit_solution(14405717227986694837)
XLA Ops:
  7.2 1.9 copy.46
  10.1 4.9 %collective-permute-start = (bf16[2,256,4,128]{3,1,2,0:T(8,128)(2,1)}, bf16[2,256,4,128]{3,1,2,0:T(8,128)(2,1)S(1)}, u32[]{:S(2)}, u32[]{:S(2)}) collective-permute-start(bf16[2,256,4,128]{3,1,2,0:T(8,128)(2,1)} %slice.23), channel_id=1, source_target_pairs={{0,2},{2,4},{4,6},{6,8},{8,10},{10,12},{12,14},{14,16},{16,18},{18... | collective-permute-start | bytes 1572872 | tf_op jit(solution)/shard_map/ppermute | solution.py:18
  15.8 4.2 collective-permute-start.1
  20.1 4.4 copy.50
  25.0 12.6 %collective-permute-done.1 = bf16[2,256,4,128]{3,1,2,0:T(8,128)(2,1)} collective-permute-done((bf16[2,256,4,128]{3,1,2,0:T(8,128)(2,1)}, bf16[2,256,4,128]{3,1,2,0:T(8,128)(2,1)}, u32[]{:S(2)}, u32[]{:S(2)}) %collective-permute-start.1) | collective-permute-done | bytes 524320 | tf_op jit(solution)/shard_map/ppermute | solution.py:18
  37.6 1.2 copy.49
  38.9 3.2 pad_maximum_fusion.1
  42.1 1.7 pad_maximum_fusion
  43.8 51.0 %while.31 = (s32[]{:T(128)}, f32[2,128,4,8]{1,3,2,0:T(8,128)S(1)}, f32[2,128,4,8,128]{1,4,3,2,0:T(8,128)}, pred[2,1280]{1,0:T(4,128)(4,1)S(1)}, s32[2,1280]{1,0:...) while((s32[]{:T(128)}, f32[2,128,4,8]{1,3,2,0:T(8,128)S(1)}, ...), condition=%wide.region_3.4_spmd, body=%wide.region_0.3_spmd.sunk | while | flops 2716145920 | bytes 71183224 | solution.py:67
  44.9 1.3 constant_dynamic-slice_fusion.3
  46.2 4.2 convolution_multiply_fusion.2
  50.4 11.6 %fusion.66 = (f32[128,4,8]{0,2,1:T(8,128)S(1)}, bf16[128,4,8,1280]{0,3,2,1:T(8,128)(2,1)}) fusion(f32[4,1280,128,8]{2,1,3,0:T(8,128)S(1)} %convolution_multiply_fusion.2, pred[128,1280]{0,1:T(8,128)(4,1)S(1)} %compare_and_fusion.3), kind=kOutput, calls=%fused_computation.85.clone.1 | output fusion | flops 26215680 | bytes 31637504 | tf_op jit(solution)/shard_map/while/body/eval_jaxpr/sub | solution.py:57
  62.1 7.3 %bitcast_dynamic-update-slice_fusion.5 = f32[2,128,4,8,128]{1,4,3,2,0:T(8,128)} fusion(f32[2,128,4,8,128]{1,4,3,2,0:T(8,128)} %get-tuple-element.439, s32[]{:T(128)} %get-tuple-element.437, bf16[128,4,8,1280]{0,3,2,1:T(8,128)(2,1)} %get-tuple-element.415, bf16[2,1280,4,128]{1,3,2,0:T(8,128)(2,1)} %get-tuple-element.455), kind=kOutput, calls=%fused_computation.19.clone.1 | convolution fusion | flops 1342177280 | bytes 13894656 | tf_op jit(solution)/shard_map/while/body/eval_jaxpr/jkgi,ikd->jkgd/dot_general | solution.py:59
  70.4 1.3 constant_dynamic-slice_fusion.3
  71.7 4.2 convolution_multiply_fusion.2
  75.9 11.6 %fusion.66 = (f32[128,4,8]{0,2,1:T(8,128)S(1)}, bf16[128,4,8,1280]{0,3,2,1:T(8,128)(2,1)}) fusion(f32[4,1280,128,8]{2,1,3,0:T(8,128)S(1)} %convolution_multiply_fusion.2, pred[128,1280]{0,1:T(8,128)(4,1)S(1)} %compare_and_fusion.3), kind=kOutput, calls=%fused_computation.85.clone.1 | output fusion | flops 26215680 | bytes 31637504 | tf_op jit(solution)/shard_map/while/body/eval_jaxpr/sub | solution.py:57
  87.5 7.3 %bitcast_dynamic-update-slice_fusion.5 = f32[2,128,4,8,128]{1,4,3,2,0:T(8,128)} fusion(f32[2,128,4,8,128]{1,4,3,2,0:T(8,128)} %get-tuple-element.439, s32[]{:T(128)} %get-tuple-element.437, bf16[128,4,8,1280]{0,3,2,1:T(8,128)(2,1)} %get-tuple-element.415, bf16[2,1280,4,128]{1,3,2,0:T(8,128)(2,1)} %get-tuple-element.455), kind=kOutput, calls=%fused_computation.19.clone.1 | convolution fusion | flops 1342177280 | bytes 13894656 | tf_op jit(solution)/shard_map/while/body/eval_jaxpr/jkgi,ikd->jkgd/dot_general | solution.py:59
  94.8 2.8 divide_convert_fusion
  97.6 3.0 copy.52
  100.6 4.3 reshape.105
  106.8 14.1 %all-gather.8.cloned.1.call-done = bf16[256,8192]{1,0:T(8,128)(2,1)} async-done(((bf16[256,4096]{1,0:T(8,128)(2,1)}), bf16[256,8192]{1,0:T(8,128)(2,1)}) %all-gather.8.cloned.1.call-update) | async-done | bytes 4194320 | tf_op jit(solution)/shard_map/all_gather | solution.py:108
  120.9 116.3 %all-gather.10.cloned.1.call-done = bf16[8192,512]{1,0:T(8,128)(2,1)} async-done(((bf16[512,512]{1,0:T(8,128)(2,1)}), bf16[8192,512]{1,0:T(8,128)(2,1)}) %all-gather.10.cloned.1.call-update) | async-done | bytes 8388624 | tf_op jit(solution)/shard_map/all_gather | solution.py:111
  237.2 7.0 %fusion.45 = bf16[256,512]{1,0:T(8,128)(2,1)S(1)} fusion(bf16[256,8192]{1,0:T(8,128)(2,1)} %all-gather.8.cloned.1.call-done, bf16[8192,512]{1,0:T(8,128)(2,1)} %all-gather.10.cloned.1.call-done), kind=kOutput, calls=%fused_computation.86 | convolution fusion | flops 2147483648 | bytes 12845056 | tf_op jit(solution)/shard_map/dot_general | solution.py:109
  244.3 106.2 %all-gather.12.cloned.1.call-done = bf16[8192,512]{1,0:T(8,128)(2,1)} async-done(((bf16[512,512]{1,0:T(8,128)(2,1)}), bf16[8192,512]{1,0:T(8,128)(2,1)}) %all-gather.12.cloned.1.call-update) | async-done | bytes 8388624 | tf_op jit(solution)/shard_map/all_gather | solution.py:116
  350.5 7.0 %fusion.46 = bf16[256,512]{1,0:T(8,128)(2,1)S(1)} fusion(bf16[256,8192]{1,0:T(8,128)(2,1)} %all-gather.8.cloned.1.call-done, bf16[8192,512]{1,0:T(8,128)(2,1)} %all-gather.12.cloned.1.call-done), kind=kOutput, calls=%fused_computation.87 | convolution fusion | flops 2147483648 | bytes 12845056 | tf_op jit(solution)/shard_map/dot_general | solution.py:114
  357.8 1.7 select_reduce_fusion
  359.5 2.1 fusion.26
  363.7 39.8 %all-gather.1 = f32[32,4,4,8]{3,2,1,0:T(4,128)S(1)} all-gather(f32[2,4,4,8]{3,2,1,0:T(4,128)S(1)} %bitcast_reduce_fusion), channel_id=3, replica_groups=mesh['seq'=16,'head'=2] {'seq'}, dimensions={0}, use_global_device_ids=true | all-gather | bytes 17408 | tf_op jit(solution)/shard_map/all_gather | solution.py:22
  403.5 38.1 %all-gather = f32[32,4,4,8]{3,2,1,0:T(4,128)S(1)} all-gather(f32[2,4,4,8]{3,2,1,0:T(4,128)S(1)} %get-tuple-element.312), channel_id=2, replica_groups=mesh['seq'=16,'head'=2] {'seq'}, dimensions={0}, use_global_device_ids=true | all-gather | bytes 17408 | tf_op jit(solution)/shard_map/all_gather | solution.py:22
  442.6 17.0 %while.32 = (s32[]{:T(128)}, f32[2,4,4,8]{3,2,1,0:T(4,128)S(1)}, f32[2,4,4,8]{3,2,1,0:T(4,128)S(1)}, f32[2,4,4,8,128]{4,3,2,1,0:T(8,128)S(1)}, f32[16,2,4,4,8]{4...) while((s32[]{:T(128)}, f32[2,4,4,8]{3,2,1,0:T(4,128)S(1)}, ...), condition=%wide.region_7.8_spmd, body=%wide.region_6.7_spmd.sunk | while | flops 99845 | bytes 403607 | solution.py:28
  459.8 2.8 fusion.47
  462.6 3.4 psum.7
  (96 shorter events, 27.2 us)
Async XLA Ops:
  7.2 350.6 %copy-start = (bf16[4,2,4,8,128]{4,3,2,1,0:T(8,128)(2,1)S(1)}, bf16[4,2,4,8,128]{4,3,2,1,0:T(8,128)(2,1)}, u32[]{:S(2)}) copy-start(bf16[4,2,4,8,128]{4,3,2,1,0:T(8,128)(2,1)} %param.26) | copy-start | bytes 196612
  7.2 7.8 %slice-start = ((bf16[2,1024,4,128]{3,2,1,0:T(4,128)(2,1)}), bf16[2,256,4,128]{3,2,1,0:T(4,128)(2,1)S(1)}, s32[]{:S(2)}) async-start(bf16[2,1024,4,128]{3,2,1,0:T(4,128)(2,1)} %param.17), calls=%async_computation.4 | async-start | bytes 1048576 | tf_op jit(solution)/shard_map/slice | solution.py:96
  7.2 12.8 %copy-start.3 = (s32[2]{0:T(128)S(1)}, s32[2]{0:T(128)}, u32[]{:S(2)}) copy-start(s32[2]{0:T(128)} %param.18) | copy-start | bytes 28
  7.2 113.7 %all-gather.8.cloned.1.call-start = ((), (), s32[]{:S(2)}) async-start(), calls=%async_computation | async-start | bytes 6291456 | tf_op jit(solution)/shard_map/all_gather | solution.py:108
  9.2 15.3 %copy-start.4 = (s32[2,16]{1,0:T(2,128)S(1)}, s32[2,16]{1,0:T(2,128)}, u32[]{:S(2)}) copy-start(s32[2,16]{1,0:T(2,128)} %param.19) | copy-start | bytes 388
  9.2 15.3 %copy-start.5 = (s32[2,16]{1,0:T(2,128)S(1)}, s32[2,16]{1,0:T(2,128)}, u32[]{:S(2)}) copy-start(s32[2,16]{1,0:T(2,128)} %param.20) | copy-start | bytes 388
  10.1 32.1 %collective-permute-start = (bf16[2,256,4,128]{3,1,2,0:T(8,128)(2,1)}, bf16[2,256,4,128]{3,1,2,0:T(8,128)(2,1)S(1)}, u32[]{:S(2)}, u32[]{:S(2)}) collective-permute-start(bf16[2,256,4,128]{3,1,2,0:T(8,128)(2,1)} %slice.23), channel_id=1, source_target_pairs={{0,2},{2,4},{4,6},{6,8},{8,10},{10,12},{12,14},{14,16},{16,18},{18... | collective-permute-start | bytes 1572872 | tf_op jit(solution)/shard_map/ppermute | solution.py:18
  15.8 21.8 %collective-permute-start.1 = (bf16[2,256,4,128]{3,1,2,0:T(8,128)(2,1)}, bf16[2,256,4,128]{3,1,2,0:T(8,128)(2,1)}, u32[]{:S(2)}, u32[]{:S(2)}) collective-permute-start(bf16[2,256,4,128]{3,1,2,0:T(8,128)(2,1)} %copy.67), channel_id=1, source_target_pairs={{0,2},{2,4},{4,6},{6,8},{8,10},{10,12},{12,14},{14,16},{16,18},{18... | collective-permute-start | bytes 1572872 | tf_op jit(solution)/shard_map/ppermute | solution.py:18
  100.6 5.8 %copy-start.1 = (bf16[2,256,4,128]{3,2,1,0:T(4,128)(2,1)S(1)}, bf16[2,256,4,128]{3,2,1,0:T(4,128)(2,1)}, u32[]{:S(2)}) copy-start(bf16[2,256,4,128]{3,2,1,0:T(4,128)(2,1)} %param.24) | copy-start | bytes 1572868
  100.6 5.9 %copy-start.2 = (bf16[2,256,4,128]{3,2,1,0:T(4,128)(2,1)S(1)}, bf16[2,256,4,128]{3,2,1,0:T(4,128)(2,1)}, u32[]{:S(2)}) copy-start(bf16[2,256,4,128]{3,2,1,0:T(4,128)(2,1)} %param.25) | copy-start | bytes 1572868
  104.9 132.3 %all-gather.10.cloned.1.call-start = ((), (), s32[]{:S(2)}) async-start(), calls=%async_computation.1 | async-start | bytes 8912896 | tf_op jit(solution)/shard_map/all_gather | solution.py:111
  105.6 244.9 %all-gather.12.cloned.1.call-start = ((), (), s32[]{:S(2)}) async-start(), calls=%async_computation.2 | async-start | bytes 8912896 | tf_op jit(solution)/shard_map/all_gather | solution.py:116
  106.4 335.3 %all-gather.14.cloned.1.call-start = ((), (), s32[]{:S(2)}) async-start(), calls=%async_computation.3 | async-start | bytes 2228224 | tf_op jit(solution)/shard_map/all_gather | solution.py:22
Sparse Core Ops, SparseCore 0:
  105.0 15.8 all-gather.7
  123.7 113.4 all-gather.9
  240.0 110.4 all-gather.11
  361.7 60.6 all-gather.13
where the time goes:
time: 474 us; the launch traced here: 473 us
  waiting for transfers between devices  250 us (53%)
  blocking collectives  81.3 us (17%)
  other arithmetic  51.1 us (11%)
  matrix products  43.6 us (9%)
  local copies, waits for them, and re-layouts  22.9 us (5%)
  between operations  14 us (3%)
  starting transfers between devices  9.39 us (2%)
    all_gather x1, waiting for transfers between devices, body(): lax.all_gather(beacon_wk, 'seq', axis=0, tiled=True)  116 us
    all_gather x1, waiting for transfers between devices, body(): lax.all_gather(beacon_wv, 'seq', axis=0, tiled=True)  106 us
    all_gather x2, blocking collectives, joined(): everything = jax.tree.map(lambda part: lax.all_gather(part, axis), shard)  78 us
    sub x2, other arithmetic, per_request(): weights = jnp.where(cache_mask, jnp.exp(scores - row_peak[..., None]), 0.0)  23.3 us
    add x15, other arithmetic, blend(): former[2] * former_scale[..., None] + latter[2] * latter_scale[..., None]  16.1 us
    dot_general x2, matrix products, per_request(): jnp.einsum('jkgi,ikd->jkgd', weights.astype(jnp.bfloat16), value_block, p...  14.5 us
    all_gather x1, waiting for transfers between devices, body(): pooled_whole = lax.all_gather(pooled_flat, 'head', axis=1, tiled=True)  14.1 us
    ppermute x2, waiting for transfers between devices, shifted(): lax.ppermute(value, axis, [(source, source + steps) for source in range(f...  12.6 us
  transfers between devices with their start and end apart: 6, of which 4 were waited for; matrix products, arithmetic and copies ran while one was open for 4% of the time, Pallas kernels for 0%

commit v1 on v0

--- a/solution.py
+++ b/solution.py
@@ -108,7 +108,9 @@
     pooled_whole = lax.all_gather(pooled_flat, "head", axis=1, tiled=True)
     key_sum = jnp.dot(
         pooled_whole,
-        lax.all_gather(beacon_wk, "seq", axis=0, tiled=True),
+        jnp.concatenate(
+            lax.all_to_all(jnp.stack([beacon_wk] * lax.axis_size("seq")), "seq", 0, 0), axis=0
+        ),
         preferred_element_type=jnp.float32,
     )
     value_sum = jnp.dot(

time: 474 us -> 536 us (1.13)
  blocking collectives: 81.3 us -> 113 us
  local copies, waits for them, and re-layouts: 22.9 us -> 50.7 us
  starting transfers between devices: 9.39 us -> 17.2 us
  waiting for transfers between devices: 250 us -> 244 us
    all_to_all x0 -> x1, waiting for transfers between devices: none -> 185 us  [body(): lax.all_to_all(jnp.stack([beacon_wk] * lax.axis_size('seq')), 'seq', 0, 0)]
    all_gather x1 -> x0, waiting for transfers between devices: 116 us -> none  [body(): lax.all_gather(beacon_wk, 'seq', axis=0, tiled=True)]
    all_gather x1, waiting for transfers between devices: 106 us -> 45.6 us  [body(): lax.all_gather(beacon_wv, 'seq', axis=0, tiled=True)]
    all_gather x2, blocking collectives: 78 us -> 109 us  [joined(): everything = jax.tree.map(lambda part: lax.all_gather(part, axis), shard)]
    all_gather x1, waiting for transfers between devices: 14.1 us -> 0.01 us  [body(): pooled_whole = lax.all_gather(pooled_flat, 'head', axis=1, tiled=True)]
    all_to_all x0 -> x1, local copies, waits for them, and re-layouts: none -> 12.3 us  [body(): lax.all_to_all(jnp.stack([beacon_wk] * lax.axis_size('seq')), 'seq', 0, 0)]
    dot_general x0 -> x1, local copies, waits for them, and re-layouts: none -> 11.4 us  [body(): jnp.dot(pooled_whole, jnp.concatenate(lax.all_to_all(jnp.stack([beacon_wk...]
    all_to_all x0 -> x1, starting transfers between devices: none -> 8.04 us  [body(): lax.all_to_all(jnp.stack([beacon_wk] * lax.axis_size('seq')), 'seq', 0, 0)]
  transfers between devices with their start and end apart: 6 -> 6, of which waited for: 4 -> 3; matrix products, arithmetic and copies ran while one was open for 4% -> 8% of each run, Pallas kernels for 0% -> 0%
where the time goes in v1:
time: 536 us; the launch traced here: 534 us
  waiting for transfers between devices  244 us (46%)
  blocking collectives  113 us (21%)
  other arithmetic  51 us (10%)
  local copies, waits for them, and re-layouts  50.7 us (9%)
  matrix products  43.6 us (8%)
  starting transfers between devices  17.2 us (3%)
  between operations  14 us (3%)
    all_to_all x1, waiting for transfers between devices, body(): lax.all_to_all(jnp.stack([beacon_wk] * lax.axis_size('seq')), 'seq', 0, 0)  185 us
    all_gather x2, blocking collectives, joined(): everything = jax.tree.map(lambda part: lax.all_gather(part, axis), shard)  109 us
    all_gather x1, waiting for transfers between devices, body(): lax.all_gather(beacon_wv, 'seq', axis=0, tiled=True)  45.6 us
    sub x2, other arithmetic, per_request(): weights = jnp.where(cache_mask, jnp.exp(scores - row_peak[..., None]), 0.0)  23.3 us
    add x15, other arithmetic, blend(): former[2] * former_scale[..., None] + latter[2] * latter_scale[..., None]  16.1 us
    dot_general x2, matrix products, per_request(): jnp.einsum('jkgi,ikd->jkgd', weights.astype(jnp.bfloat16), value_block, p...  14.6 us
    ppermute x2, waiting for transfers between devices, shifted(): lax.ppermute(value, axis, [(source, source + steps) for source in range(f...  12.6 us
    all_to_all x1, local copies, waits for them, and re-layouts, body(): lax.all_to_all(jnp.stack([beacon_wk] * lax.axis_size('seq')), 'seq', 0, 0)  12.3 us
  transfers between devices with their start and end apart: 6, of which 3 were waited for; matrix products, arithmetic and copies ran while one was open for 8% of the time, Pallas kernels for 0%

profile of v1, /device:TPU:0, one launch (start us, length us, event | category | flops | bytes accessed | tf_op | source)
XLA Modules:
  0.0 533.8 jit_solution(11767406764172127933)
XLA Ops:
  7.2 1.9 copy.61
  10.0 4.9 collective-permute-start
  15.8 4.2 collective-permute-start.1
  20.1 4.4 copy.65
  25.0 12.6 %collective-permute-done.1 = bf16[2,256,4,128]{3,1,2,0:T(8,128)(2,1)} collective-permute-done((bf16[2,256,4,128]{3,1,2,0:T(8,128)(2,1)}, bf16[2,256,4,128]{3,1,2,0:T(8,128)(2,1)}, u32[]{:S(2)}, u32[]{:S(2)}) %collective-permute-start.1) | collective-permute-done | bytes 524320 | tf_op jit(solution)/shard_map/ppermute | solution.py:18
  38.9 3.3 pad_maximum_fusion.1
  42.1 1.7 pad_maximum_fusion
  43.8 51.0 %while.31 = (s32[]{:T(128)}, f32[2,128,4,8]{1,3,2,0:T(8,128)S(1)}, f32[2,128,4,8,128]{1,4,3,2,0:T(8,128)}, pred[2,1280]{1,0:T(4,128)(4,1)S(1)}, s32[2,1280]{1,0:...) while((s32[]{:T(128)}, f32[2,128,4,8]{1,3,2,0:T(8,128)S(1)}, ...), condition=%wide.region_3.4_spmd, body=%wide.region_0.3_spmd.sunk | while | flops 2716145920 | bytes 71183224 | solution.py:67
  46.2 4.2 convolution_multiply_fusion.2
  50.4 11.6 %fusion.65 = (f32[128,4,8]{0,2,1:T(8,128)S(1)}, bf16[128,4,8,1280]{0,3,2,1:T(8,128)(2,1)}) fusion(f32[4,1280,128,8]{2,1,3,0:T(8,128)S(1)} %convolution_multiply_fusion.2, pred[128,1280]{0,1:T(8,128)(4,1)S(1)} %compare_and_fusion.3), kind=kOutput, calls=%fused_computation.85.clone.1 | output fusion | flops 26215680 | bytes 31637504 | tf_op jit(solution)/shard_map/while/body/eval_jaxpr/sub | solution.py:57
  62.1 7.2 %bitcast_dynamic-update-slice_fusion.5 = f32[2,128,4,8,128]{1,4,3,2,0:T(8,128)} fusion(f32[2,128,4,8,128]{1,4,3,2,0:T(8,128)} %get-tuple-element.449, s32[]{:T(128)} %get-tuple-element.447, bf16[128,4,8,1280]{0,3,2,1:T(8,128)(2,1)} %get-tuple-element.425, bf16[2,1280,4,128]{1,3,2,0:T(8,128)(2,1)} %get-tuple-element.465), kind=kOutput, calls=%fused_computation.19.clone.1 | convolution fusion | flops 1342177280 | bytes 13894656 | tf_op jit(solution)/shard_map/while/body/eval_jaxpr/jkgi,ikd->jkgd/dot_general | solution.py:59
  71.6 4.2 convolution_multiply_fusion.2
  75.9 11.6 %fusion.65 = (f32[128,4,8]{0,2,1:T(8,128)S(1)}, bf16[128,4,8,1280]{0,3,2,1:T(8,128)(2,1)}) fusion(f32[4,1280,128,8]{2,1,3,0:T(8,128)S(1)} %convolution_multiply_fusion.2, pred[128,1280]{0,1:T(8,128)(4,1)S(1)} %compare_and_fusion.3), kind=kOutput, calls=%fused_computation.85.clone.1 | output fusion | flops 26215680 | bytes 31637504 | tf_op jit(solution)/shard_map/while/body/eval_jaxpr/sub | solution.py:57
  87.5 7.3 %bitcast_dynamic-update-slice_fusion.5 = f32[2,128,4,8,128]{1,4,3,2,0:T(8,128)} fusion(f32[2,128,4,8,128]{1,4,3,2,0:T(8,128)} %get-tuple-element.449, s32[]{:T(128)} %get-tuple-element.447, bf16[128,4,8,1280]{0,3,2,1:T(8,128)(2,1)} %get-tuple-element.425, bf16[2,1280,4,128]{1,3,2,0:T(8,128)(2,1)} %get-tuple-element.465), kind=kOutput, calls=%fused_computation.19.clone.1 | convolution fusion | flops 1342177280 | bytes 13894656 | tf_op jit(solution)/shard_map/while/body/eval_jaxpr/jkgi,ikd->jkgd/dot_general | solution.py:59
  94.8 2.8 divide_convert_fusion
  97.6 3.0 copy.67
  100.6 4.2 reshape.110
  105.1 4.0 stack.2
  109.2 8.0 %all-to-all-start = ((bf16[16,512,512]{1,2,0:T(8,128)(2,1)}), bf16[16,512,512]{1,2,0:T(8,128)(2,1)}, u32[]{:S(2)}, u32[]{:S(2)}) async-start(bf16[16,512,512]{1,2,0:T(8,128)(2,1)} %stack.2), calls=%async_computation | async-start | bytes 16777216 | tf_op jit(solution)/shard_map/all_to_all | solution.py:112
  118.4 185.3 %all-to-all-done = bf16[16,512,512]{1,2,0:T(8,128)(2,1)} async-done(((bf16[16,512,512]{1,2,0:T(8,128)(2,1)}), bf16[16,512,512]{1,2,0:T(8,128)(2,1)}, u32[]{:S(2)}, u32[]{:S(2)}) %all-to-all-start) | async-done | bytes 8388640 | tf_op jit(solution)/shard_map/all_to_all | solution.py:112
  303.7 12.3 %copy.69 = bf16[16,512,512]{2,1,0:T(8,128)(2,1)} copy(bf16[16,512,512]{1,2,0:T(8,128)(2,1)} %all-to-all-done) | data formatting | bytes 16777216 | tf_op jit(solution)/shard_map/all_to_all | solution.py:112
  316.0 11.4 %copy.70 = bf16[512,8192]{1,0:T(8,128)(2,1)} copy(bf16[512,8192]{0,1:T(8,128)(2,1)} %bitcast.115) | data formatting | bytes 16777216 | tf_op jit(solution)/shard_map/dot_general | solution.py:109
  327.4 45.6 %all-gather.9.cloned.1.call-done = bf16[8192,512]{1,0:T(8,128)(2,1)} async-done(((bf16[512,512]{1,0:T(8,128)(2,1)}), bf16[8192,512]{1,0:T(8,128)(2,1)}) %all-gather.9.cloned.1.call-update) | async-done | bytes 8388624 | tf_op jit(solution)/shard_map/all_gather | solution.py:118
  372.9 7.0 %fusion.45 = bf16[256,512]{1,0:T(8,128)(2,1)S(1)} fusion(bf16[256,8192]{1,0:T(8,128)(2,1)} %all-gather.7.cloned.1.call-done, bf16[8192,512]{1,0:T(8,128)(2,1)} %all-gather.9.cloned.1.call-done), kind=kOutput, calls=%fused_computation.86 | convolution fusion | flops 2147483648 | bytes 12845056 | tf_op jit(solution)/shard_map/dot_general | solution.py:116
  380.1 7.0 %fusion.32 = bf16[2,128,4,128]{3,1,2,0:T(8,128)(2,1)S(1)} fusion(bf16[2,128,8192,1]{2,1,3,0:T(8,128)(2,1)} %bitcast.120, bf16[4,128,8192,1]{2,1,0,3:T(8,128)(2,1)} %bitcast.116, pred[2,128]{1,0:T(4,128)(4,1)S(1)} %iota_compare_fusion.1), kind=kOutput, calls=%fused_computation.52 | convolution fusion | flops 2147745792 | bytes 12845312 | tf_op jit(solution)/shard_map/dot_general | solution.py:109
  387.2 1.7 select_reduce_fusion
  388.9 2.1 fusion.26
  393.1 71.1 %all-gather.1 = f32[32,4,4,8]{3,2,1,0:T(4,128)S(1)} all-gather(f32[2,4,4,8]{3,2,1,0:T(4,128)S(1)} %bitcast_reduce_fusion), channel_id=3, replica_groups=mesh['seq'=16,'head'=2] {'seq'}, dimensions={0}, use_global_device_ids=true | all-gather | bytes 17408 | tf_op jit(solution)/shard_map/all_gather | solution.py:22
  464.2 38.2 %all-gather = f32[32,4,4,8]{3,2,1,0:T(4,128)S(1)} all-gather(f32[2,4,4,8]{3,2,1,0:T(4,128)S(1)} %get-tuple-element.322), channel_id=2, replica_groups=mesh['seq'=16,'head'=2] {'seq'}, dimensions={0}, use_global_device_ids=true | all-gather | bytes 17408 | tf_op jit(solution)/shard_map/all_gather | solution.py:22
  503.3 17.0 %while.32 = (s32[]{:T(128)}, f32[2,4,4,8]{3,2,1,0:T(4,128)S(1)}, f32[2,4,4,8]{3,2,1,0:T(4,128)S(1)}, f32[2,4,4,8,128]{4,3,2,1,0:T(8,128)S(1)}, f32[16,2,4,4,8]{4...) while((s32[]{:T(128)}, f32[2,4,4,8]{3,2,1,0:T(4,128)S(1)}, ...), condition=%wide.region_7.8_spmd, body=%wide.region_6.7_spmd.sunk | while | flops 99845 | bytes 403607 | solution.py:28
  520.5 2.8 fusion.46
  523.3 3.4 psum.7
  (100 shorter events, 30.4 us)
Async XLA Ops:
  7.2 380.0 %copy-start = (bf16[4,2,4,8,128]{4,3,2,1,0:T(8,128)(2,1)S(1)}, bf16[4,2,4,8,128]{4,3,2,1,0:T(8,128)(2,1)}, u32[]{:S(2)}) copy-start(bf16[4,2,4,8,128]{4,3,2,1,0:T(8,128)(2,1)} %param.26) | copy-start | bytes 196612
  7.2 7.8 %slice-start = ((bf16[2,1024,4,128]{3,2,1,0:T(4,128)(2,1)}), bf16[2,256,4,128]{3,2,1,0:T(4,128)(2,1)S(1)}, s32[]{:S(2)}) async-start(bf16[2,1024,4,128]{3,2,1,0:T(4,128)(2,1)} %param.17), calls=%async_computation.4 | async-start | bytes 1048576 | tf_op jit(solution)/shard_map/slice | solution.py:96
  7.2 12.8 %copy-start.4 = (s32[2]{0:T(128)S(1)}, s32[2]{0:T(128)}, u32[]{:S(2)}) copy-start(s32[2]{0:T(128)} %param.18) | copy-start | bytes 28
  7.2 320.2 %all-gather.7.cloned.1.call-start = ((), (), s32[]{:S(2)}) async-start(), calls=%async_computation.1 | async-start | bytes 6291456 | tf_op jit(solution)/shard_map/all_gather | solution.py:108
  9.2 15.3 %copy-start.5 = (s32[2,16]{1,0:T(2,128)S(1)}, s32[2,16]{1,0:T(2,128)}, u32[]{:S(2)}) copy-start(s32[2,16]{1,0:T(2,128)} %param.19) | copy-start | bytes 388
  9.2 15.3 %copy-start.6 = (s32[2,16]{1,0:T(2,128)S(1)}, s32[2,16]{1,0:T(2,128)}, u32[]{:S(2)}) copy-start(s32[2,16]{1,0:T(2,128)} %param.20) | copy-start | bytes 388
  10.0 32.1 %collective-permute-start = (bf16[2,256,4,128]{3,1,2,0:T(8,128)(2,1)}, bf16[2,256,4,128]{3,1,2,0:T(8,128)(2,1)S(1)}, u32[]{:S(2)}, u32[]{:S(2)}) collective-permute-start(bf16[2,256,4,128]{3,1,2,0:T(8,128)(2,1)} %slice.23), channel_id=1, source_target_pairs={{0,2},{2,4},{4,6},{6,8},{8,10},{10,12},{12,14},{14,16},{16,18},{18... | collective-permute-start | bytes 1572872 | tf_op jit(solution)/shard_map/ppermute | solution.py:18
  15.8 21.8 %collective-permute-start.1 = (bf16[2,256,4,128]{3,1,2,0:T(8,128)(2,1)}, bf16[2,256,4,128]{3,1,2,0:T(8,128)(2,1)}, u32[]{:S(2)}, u32[]{:S(2)}) collective-permute-start(bf16[2,256,4,128]{3,1,2,0:T(8,128)(2,1)} %copy.85), channel_id=1, source_target_pairs={{0,2},{2,4},{4,6},{6,8},{8,10},{10,12},{12,14},{14,16},{16,18},{18... | collective-permute-start | bytes 1572872 | tf_op jit(solution)/shard_map/ppermute | solution.py:18
  100.6 4.3 copy-start.1
  109.2 8.9 %copy-start.2 = (bf16[2,256,4,128]{3,2,1,0:T(4,128)(2,1)S(1)}, bf16[2,256,4,128]{3,2,1,0:T(4,128)(2,1)}, u32[]{:S(2)}) copy-start(bf16[2,256,4,128]{3,2,1,0:T(4,128)(2,1)} %param.24) | copy-start | bytes 1572868
  109.2 8.9 %copy-start.3 = (bf16[2,256,4,128]{3,2,1,0:T(4,128)(2,1)S(1)}, bf16[2,256,4,128]{3,2,1,0:T(4,128)(2,1)}, u32[]{:S(2)}) copy-start(bf16[2,256,4,128]{3,2,1,0:T(4,128)(2,1)} %param.25) | copy-start | bytes 1572868
  109.2 194.6 %all-to-all-start = ((bf16[16,512,512]{1,2,0:T(8,128)(2,1)}), bf16[16,512,512]{1,2,0:T(8,128)(2,1)}, u32[]{:S(2)}, u32[]{:S(2)}) async-start(bf16[16,512,512]{1,2,0:T(8,128)(2,1)} %stack.2), calls=%async_computation | async-start | bytes 16777216 | tf_op jit(solution)/shard_map/all_to_all | solution.py:112
  117.2 255.7 %all-gather.9.cloned.1.call-start = ((), (), s32[]{:S(2)}) async-start(), calls=%async_computation.2 | async-start | bytes 8912896 | tf_op jit(solution)/shard_map/all_gather | solution.py:118
  118.0 384.4 %all-gather.11.cloned.1.call-start = ((), (), s32[]{:S(2)}) async-start(), calls=%async_computation.3 | async-start | bytes 2228224 | tf_op jit(solution)/shard_map/all_gather | solution.py:22
Sparse Core Ops, SparseCore 0:
  105.0 15.8 all-gather.6
  123.7 249.1 all-gather.8
  391.1 92.1 all-gather.10
